TPU v7x, 32 devices: a whole 2x2x4 slice. The times are simulated.
32 devices in a mesh: dom: 8 (over z, y), batch: 4 (over x, core).
Axes of the slice: x: 2, y: 2, z: 4, core: 2. Of those that a mesh axis runs over, the one named last changes fastest.
Arguments:
- signal: bfloat16 [4096, 4, 4, 256], P('dom', 'batch'), may hold values from -6 to 6
- cotangent: bfloat16 [4096, 4, 3, 256], P('dom', 'batch'), may hold values from -6 to 6
- conv_weight: bfloat16 [2, 2, 256, 256], replicated, may hold values from -0.25 to 0.25
- mix_weight: bfloat16 [3, 256, 256], replicated, may hold values from -0.21875 to 0.21875
- send_rows: int32 [64, 16], P('dom'), may hold values from 0 to 511
- send_mask: int32 [64, 16], P('dom'), may hold values 0 or 1
- tile_vals: bfloat16 [128, 128, 128], P('dom'), may hold values from -0.26953125 to 0.26953125
- tile_row: int32 [128], P('dom'), may hold values from 0 to 3
- tile_col: int32 [128], P('dom'), may hold values from 0 to 5
- tile_mask: int32 [128], P('dom'), may hold values 0 or 1
- hub_owner: int32 [8], replicated, may hold values from 0 to 7, as said below
- hub_rows: int32 [8, 16], replicated, may hold values from 0 to 511
Outputs:
- layer_out: bfloat16 [4096, 4, 3, 256], P('dom', 'batch')
- signal_grad: bfloat16 [4096, 4, 4, 256], P('dom', 'batch')
- conv_grad: float32 [2, 2, 256, 256], replicated
- mix_grad: float32 [3, 256, 256], replicated
Inputs may be any that keep to these rules, and one draw needn't show every extreme that they name: `hub_owner`: each owner slot names a different partition.
All inputs are finite; a program needn't handle non-finite values. No bound on the sum of `send_mask` or of `tile_mask` on one device may be relied on, other than what follows from the above.
Results may differ from a plain program's by a relative error of at most 0.0056.
Values may be sent and summed in bfloat16 or wider, within the bound.
A program may use at most 128 MiB of HBM per device.

v0:
```python
import math
import jax
import jax.numpy as jnp
from jax import lax
from jax.sharding import PartitionSpec as P

highest = lax.Precision.HIGHEST


def tile_apply(ext_rows, tile_block, row_ids, col_ids, tile_keep, row_tiles):
    block_rows = tile_block.shape[1]
    features = ext_rows.shape[1]
    chosen = ext_rows.reshape(-1, block_rows, features)[col_ids]
    product = jnp.einsum("tij,tjf->tif", tile_block, chosen, preferred_element_type=jnp.float32)
    product = product * tile_keep[:, None, None]
    onehot = (row_ids[None, :] == jnp.arange(row_tiles, dtype=jnp.int32)[:, None]).astype(
        jnp.float32
    )
    return jnp.einsum("rt,tif->rif", onehot, product, precision=highest).reshape(
        row_tiles * block_rows, features
    )


def tile_back(own_rows, tile_block, row_ids, col_ids, tile_keep, col_tiles):
    block_rows = tile_block.shape[1]
    features = own_rows.shape[1]
    chosen = own_rows.reshape(-1, block_rows, features)[row_ids]
    product = jnp.einsum("tji,tjf->tif", tile_block, chosen, preferred_element_type=jnp.float32)
    product = product * tile_keep[:, None, None]
    onehot = (col_ids[None, :] == jnp.arange(col_tiles, dtype=jnp.int32)[:, None]).astype(
        jnp.float32
    )
    return jnp.einsum("ct,tif->cif", onehot, product, precision=highest).reshape(
        col_tiles * block_rows, features
    )


def mm(left, right):
    return jnp.dot(left, right, preferred_element_type=jnp.float32)


def inner_sum(left, right):
    return lax.dot_general(
        left, right, (((0,), (0,)), ((), ())), preferred_element_type=jnp.float32
    )


def body(
    signal,
    cotangent,
    conv_weight,
    mix_weight,
    send_rows,
    send_mask,
    tile_vals,
    tile_row,
    tile_col,
    tile_mask,
    hub_owner,
    hub_rows,
):
    node_dev, b_dev, steps, chans = signal.shape
    out_steps = steps - 1
    block_rows = tile_vals.shape[1]
    features = b_dev * out_steps * chans
    halo_count = send_rows.shape[0] * send_rows.shape[1]
    hub_count = hub_rows.shape[0] * hub_rows.shape[1]
    ext_count = node_dev + halo_count + hub_count
    my_index = lax.axis_index("dom")
    flat_send = send_rows.reshape(-1)
    send_flag = send_mask.reshape(-1)
    keep_send = send_flag.astype(jnp.bfloat16)
    flat_hub = hub_rows.reshape(-1)
    mine = jnp.repeat(hub_owner, hub_rows.shape[1]) == my_index
    positions = jnp.arange(node_dev, dtype=jnp.int32)
    return_halo = ((positions[:, None] == flat_send[None, :]) & (send_flag[None, :] == 1)).astype(
        jnp.float32
    )
    return_hub = ((positions[:, None] == flat_hub[None, :]) & mine[None, :]).astype(jnp.float32)
    tile_keep = tile_mask.astype(jnp.float32)

    def spread(field):
        outgoing = field[flat_send] * keep_send[:, None]
        incoming = lax.all_to_all(outgoing, "dom", split_axis=0, concat_axis=0, tiled=True)
        placed = jnp.where(
            mine[:, None], field[flat_hub].astype(jnp.float32), jnp.zeros((), jnp.float32)
        )
        hubs = lax.psum(placed, "dom").astype(jnp.bfloat16)
        ext_rows = jnp.concatenate([field, incoming, hubs], 0)
        return tile_apply(
            ext_rows, tile_vals, tile_row, tile_col, tile_keep, node_dev // block_rows
        )

    def gather_back(field):
        ext_grad = tile_back(
            field, tile_vals, tile_row, tile_col, tile_keep, ext_count // block_rows
        )
        returned = lax.all_to_all(
            ext_grad[node_dev : node_dev + halo_count].astype(jnp.bfloat16),
            "dom",
            split_axis=0,
            concat_axis=0,
            tiled=True,
        ).astype(jnp.float32)
        summed = lax.psum(ext_grad[node_dev + halo_count :], "dom")
        local = ext_grad[:node_dev] + jnp.dot(return_halo, returned, precision=highest)
        return local + jnp.dot(return_hub, summed, precision=highest)

    earlier = signal[:, :, :-1, :].reshape(-1, chans)
    later = signal[:, :, 1:, :].reshape(-1, chans)
    filt = mm(earlier, conv_weight[0, 0]) + mm(later, conv_weight[0, 1])
    gate = mm(earlier, conv_weight[1, 0]) + mm(later, conv_weight[1, 1])
    tanh_filt = jnp.tanh(filt)
    sig_gate = jax.nn.sigmoid(gate)
    hidden = (tanh_filt * sig_gate).astype(jnp.bfloat16)
    hop_one = spread(hidden.reshape(node_dev, features)).astype(jnp.bfloat16)
    hop_two = spread(hop_one).astype(jnp.bfloat16)
    hop_one = hop_one.reshape(-1, chans)
    hop_two = hop_two.reshape(-1, chans)
    mixed = (
        later.astype(jnp.float32)
        + mm(hidden, mix_weight[0])
        + mm(hop_one, mix_weight[1])
        + mm(hop_two, mix_weight[2])
    )
    layer_out = mixed.astype(jnp.bfloat16).reshape(node_dev, b_dev, out_steps, chans)
    grad_out = cotangent.reshape(-1, chans)
    mix_part = jnp.stack(
        [inner_sum(hidden, grad_out), inner_sum(hop_one, grad_out), inner_sum(hop_two, grad_out)]
    )
    back_two = mm(grad_out, mix_weight[2].T).astype(jnp.bfloat16)
    back_one = mm(grad_out, mix_weight[1].T) + gather_back(
        back_two.reshape(node_dev, features)
    ).reshape(-1, chans)
    back_one = back_one.astype(jnp.bfloat16)
    grad_hidden = mm(grad_out, mix_weight[0].T) + gather_back(
        back_one.reshape(node_dev, features)
    ).reshape(-1, chans)
    grad_filt = (grad_hidden * sig_gate * (1.0 - tanh_filt * tanh_filt)).astype(jnp.bfloat16)
    grad_gate = (grad_hidden * tanh_filt * sig_gate * (1.0 - sig_gate)).astype(jnp.bfloat16)
    conv_part = jnp.stack(
        [
            jnp.stack([inner_sum(earlier, grad_filt), inner_sum(later, grad_filt)]),
            jnp.stack([inner_sum(earlier, grad_gate), inner_sum(later, grad_gate)]),
        ]
    )
    shape_four = (node_dev, b_dev, out_steps, chans)
    into_earlier = (
        mm(grad_filt, conv_weight[0, 0].T) + mm(grad_gate, conv_weight[1, 0].T)
    ).reshape(shape_four)
    into_later = (
        mm(grad_filt, conv_weight[0, 1].T)
        + mm(grad_gate, conv_weight[1, 1].T)
        + grad_out.astype(jnp.float32)
    ).reshape(shape_four)
    signal_grad = jnp.pad(into_earlier, ((0, 0), (0, 0), (0, 1), (0, 0))) + jnp.pad(
        into_later, ((0, 0), (0, 0), (1, 0), (0, 0))
    )
    conv_total, mix_total = lax.psum((conv_part, mix_part), ("dom", "batch"))
    factor = 1.0 / math.sqrt(
        node_dev * lax.axis_size("dom") * b_dev * lax.axis_size("batch") * out_steps
    )
    return (layer_out, signal_grad.astype(jnp.bfloat16), conv_total * factor, mix_total * factor)


def solution(mesh):
    placed = (
        P("dom", "batch", None, None),
        P("dom", "batch", None, None),
        P(),
        P(),
        P("dom", None),
        P("dom", None),
        P("dom", None, None),
        P("dom"),
        P("dom"),
        P("dom"),
        P(),
        P(),
    )
    return jax.shard_map(
        body,
        mesh=mesh,
        in_specs=placed,
        out_specs=(P("dom", "batch", None, None), P("dom", "batch", None, None), P(), P()),
        check_vma=False,
    )
```

profile of v0, /device:TPU:0, one launch (start us, length us, event | category | flops | bytes accessed | tf_op | source)
XLA Modules:
  0.0 550.8 jit_solution(4992081128185602620)
XLA Ops:
  14.0 5.6 %fusion.96 = f32[16,768,128]{2,1,0:T(8,128)} fusion(bf16[16,128,768]{2,1,0:T(8,128)(2,1)} %gather_fusion.6, bf16[16,128,128]{2,1,0:T(8,128)(2,1)S(1)} %copy-done), kind=kOutput, calls=%fused_computation.145 | convolution fusion | flops 402653184 | bytes 9961472 | tf_op jit(solution)/shard_map/tji,tjf->tif/dot_general | solution.py:28
  19.5 6.7 %copy.32 = f32[16,768,128]{1,0,2:T(8,128)} copy(f32[16,768,128]{2,1,0:T(8,128)} %fusion.96) | data formatting | bytes 12582912 | tf_op jit(solution)/shard_map/tji,tjf->tif/dot_general | solution.py:28
  26.3 4.6 fusion.2
  36.8 7.3 %all-to-all-start.2 = ((bf16[8,16,768]{2,1,0:T(8,128)(2,1)}), bf16[8,16,768]{2,1,0:T(8,128)(2,1)}, u32[]{:S(2)}, u32[]{:S(2)}) async-start(bf16[8,16,768]{2,1,0:T(8,128)(2,1)} %bitcast.44), calls=%async_computation.2 | async-start | bytes 393216 | tf_op jit(solution)/shard_map/all_to_all | solution.py:98
  60.6 49.4 %all-reduce.9.cloned.1.call-done = f32[128,768]{1,0:T(8,128)} async-done(((f32[128,768]{1,0:T(8,128)}), f32[128,768]{1,0:T(8,128)}) %all-reduce.9.cloned.1.call-update) | async-done | bytes 393232 | tf_op jit(solution)/shard_map/psum | solution.py:105
  125.7 5.6 %fusion.97 = f32[16,768,128]{2,1,0:T(8,128)} fusion(bf16[16,128,768]{2,1,0:T(8,128)(2,1)} %gather_fusion.7, bf16[16,128,128]{2,1,0:T(8,128)(2,1)S(1)} %copy-done), kind=kOutput, calls=%fused_computation.146 | convolution fusion | flops 402653184 | bytes 9961472 | tf_op jit(solution)/shard_map/tji,tjf->tif/dot_general | solution.py:28
  131.3 6.7 %copy.33 = f32[16,768,128]{1,0,2:T(8,128)} copy(f32[16,768,128]{2,1,0:T(8,128)} %fusion.97) | data formatting | bytes 12582912 | tf_op jit(solution)/shard_map/tji,tjf->tif/dot_general | solution.py:28
  138.0 4.6 fusion
  149.9 4.1 all-to-all-start.3
  157.0 60.8 %all-reduce.11.cloned.1.call-done = f32[128,768]{1,0:T(8,128)} async-done(((f32[128,768]{1,0:T(8,128)}), f32[128,768]{1,0:T(8,128)}) %all-reduce.11.cloned.1.call-update) | async-done | bytes 393232 | tf_op jit(solution)/shard_map/psum | solution.py:105
  242.7 40.9 %all-reduce.14 = bf16[128,768]{1,0:T(8,128)(2,1)} all-reduce(f32[128,768]{1,0:T(8,128)} %convert_select_fusion.1), channel_id=1, replica_groups=mesh['dom'=8,'batch'=4] {'dom'}, use_global_device_ids=true, to_apply=%region_0.1 | all-reduce | flops 98304 | bytes 589824 | tf_op jit(solution)/shard_map/psum | solution.py:88
  286.8 4.2 all-to-all-start
  297.2 3.6 reshape.189
  300.8 3.6 reshape.190
  304.4 4.0 fusion.32
  313.0 5.6 %fusion.94 = f32[16,768,128]{2,1,0:T(8,128)} fusion(bf16[16,128,768]{2,1,0:T(8,128)(2,1)} %gather_fusion.2, bf16[16,128,128]{2,1,0:T(8,128)(2,1)S(1)} %copy-done), kind=kOutput, calls=%fused_computation.143 | convolution fusion | flops 402653184 | bytes 9961472 | tf_op jit(solution)/shard_map/tij,tjf->tif/dot_general | solution.py:14
  318.6 6.7 %copy.30 = f32[16,768,128]{1,0,2:T(8,128)} copy(f32[16,768,128]{2,1,0:T(8,128)} %fusion.94) | data formatting | bytes 12582912 | tf_op jit(solution)/shard_map/tij,tjf->tif/dot_general | solution.py:14
  325.3 5.6 %fusion.26 = bf16[4,128,768]{2,0,1:T(4,128)(2,1)S(1)} fusion(f32[16,768,128]{1,0,2:T(8,128)} %copy.30, f32[16]{0:T(128)S(1)} %convert_element_type.95, s32[16]{0:T(128)S(1)} %copy-done.30), kind=kOutput, calls=%fused_computation.50 | convolution fusion | flops 77463616 | bytes 7078016 | tf_op jit(solution)/shard_map/rt,tif->rif/dot_general | solution.py:19
  335.8 6.0 %all-to-all-start.1 = ((bf16[8,16,768]{2,1,0:T(8,128)(2,1)}), bf16[8,16,768]{2,1,0:T(8,128)(2,1)S(1)}, u32[]{:S(2)}, u32[]{:S(2)}) async-start(bf16[8,16,768]{2,1,0:T(8,128)(2,1)} %broadcast_multiply_fusion.2), calls=%async_computation.1 | async-start | bytes 393216 | tf_op jit(solution)/shard_map/all_to_all | solution.py:84
  341.8 42.5 %all-reduce.15 = bf16[128,768]{1,0:T(8,128)(2,1)} all-reduce(f32[128,768]{1,0:T(8,128)S(1)} %convert_select_fusion), channel_id=1, replica_groups=mesh['dom'=8,'batch'=4] {'dom'}, use_global_device_ids=true, to_apply=%region_1.2 | all-reduce | flops 98304 | bytes 589824 | tf_op jit(solution)/shard_map/psum | solution.py:88
  388.8 5.6 %fusion.95 = f32[16,768,128]{2,1,0:T(8,128)} fusion(bf16[16,128,768]{2,1,0:T(8,128)(2,1)} %gather_fusion.5, bf16[16,128,128]{2,1,0:T(8,128)(2,1)S(1)} %copy-done), kind=kOutput, calls=%fused_computation.144 | convolution fusion | flops 402653184 | bytes 9961472 | tf_op jit(solution)/shard_map/tij,tjf->tif/dot_general | solution.py:14
  394.4 6.7 %copy.31 = f32[16,768,128]{1,0,2:T(8,128)} copy(f32[16,768,128]{2,1,0:T(8,128)} %fusion.95) | data formatting | bytes 12582912 | tf_op jit(solution)/shard_map/tij,tjf->tif/dot_general | solution.py:14
  401.1 5.6 %fusion.29 = bf16[4,128,768]{2,0,1:T(4,128)(2,1)S(1)} fusion(f32[16,768,128]{1,0,2:T(8,128)} %copy.31, f32[16]{0:T(128)S(1)} %convert_element_type.95, s32[16]{0:T(128)S(1)} %copy-done.30), kind=kOutput, calls=%fused_computation.51 | convolution fusion | flops 77463616 | bytes 7078016 | tf_op jit(solution)/shard_map/rt,tif->rif/dot_general | solution.py:19
  413.2 127.3 %all-reduce.13.cloned.1.call-done = (f32[2,2,256,256]{2,3,1,0:T(8,128)}, f32[3,256,256]{2,1,0:T(8,128)}) async-done(((f32[2,2,256,256]{2,3,1,0:T(8,128)}, f32[3,256,256]{2,1,0:T(8,128)}), (f32[2,2,256,256]{2,3,1,0:T(8,128)}, f32[3,256,256]{2,1,0:T(8,128)})) %all-reduce.13.cloned.1.call-update) | async-done | bytes 1835024 | tf_op jit(solution)/shard_map/psum | solution.py:159
  (169 shorter events, 113.1 us)
Async XLA Ops:
  7.2 6.8 %copy-start = (bf16[16,128,128]{2,1,0:T(8,128)(2,1)S(1)}, bf16[16,128,128]{2,1,0:T(8,128)(2,1)}, u32[]{:S(2)}) copy-start(bf16[16,128,128]{2,1,0:T(8,128)(2,1)} %param.18) | copy-start | bytes 1572868
  7.2 102.8 %all-reduce.9.cloned.1.call-start = ((), (), s32[]{:S(2)}) async-start(), calls=%async_computation.4 | async-start | bytes 786432 | tf_op jit(solution)/shard_map/psum | solution.py:105
  19.5 6.7 %copy-start.31 = (s32[16]{0:T(128)S(1)}, s32[16]{0:T(128)}, u32[]{:S(2)}) copy-start(s32[16]{0:T(128)} %param.21) | copy-start | bytes 196
  19.5 6.7 %copy-start.29 = (s32[16]{0:T(128)S(1)}, s32[16]{0:T(128)}, u32[]{:S(2)}) copy-start(s32[16]{0:T(128)} %param.20) | copy-start | bytes 196
  36.8 76.2 %all-to-all-start.2 = ((bf16[8,16,768]{2,1,0:T(8,128)(2,1)}), bf16[8,16,768]{2,1,0:T(8,128)(2,1)}, u32[]{:S(2)}, u32[]{:S(2)}) async-start(bf16[8,16,768]{2,1,0:T(8,128)(2,1)} %bitcast.44), calls=%async_computation.2 | async-start | bytes 393216 | tf_op jit(solution)/shard_map/all_to_all | solution.py:98
  44.1 173.7 %all-reduce.11.cloned.1.call-start = ((), (), s32[]{:S(2)}) async-start(), calls=%async_computation.5 | async-start | bytes 786432 | tf_op jit(solution)/shard_map/psum | solution.py:105
  44.4 3.4 copy-start.27
  44.4 3.5 copy-start.28
  44.4 3.7 copy-start.26
  44.5 3.7 copy-start.32
  48.3 3.1 copy-start.7
  53.5 5.2 copy-start.14
  55.9 3.1 copy-start.3
  149.9 70.8 %all-to-all-start.3 = ((bf16[8,16,768]{2,1,0:T(8,128)(2,1)}), bf16[8,16,768]{2,1,0:T(8,128)(2,1)S(1)}, u32[]{:S(2)}, u32[]{:S(2)}) async-start(bf16[8,16,768]{2,1,0:T(8,128)(2,1)} %bitcast.46), calls=%async_computation.3 | async-start | bytes 393216 | tf_op jit(solution)/shard_map/all_to_all | solution.py:98
  226.8 2.0 copy-start.4
  226.8 2.2 copy-start.15
  226.8 2.7 copy-start.17
  231.4 2.2 copy-start.10
  286.8 22.7 %all-to-all-start = ((bf16[8,16,768]{2,1,0:T(8,128)(2,1)}), bf16[8,16,768]{2,1,0:T(8,128)(2,1)}, u32[]{:S(2)}, u32[]{:S(2)}) async-start(bf16[8,16,768]{2,1,0:T(8,128)(2,1)} %broadcast_multiply_fusion.3), calls=%async_computation | async-start | bytes 393216 | tf_op jit(solution)/shard_map/all_to_all | solution.py:84
  291.0 3.4 copy-start.6
  291.0 3.4 copy-start.11
  333.8 51.6 %copy-start.12 = (bf16[1536,256]{1,0:T(8,128)(2,1)}, bf16[1536,256]{1,0:T(8,128)(2,1)S(1)}, u32[]{:S(2)}) copy-start(bf16[1536,256]{1,0:T(8,128)(2,1)S(1)} %convert_element_type.97) | copy-start | bytes 2359300
  335.8 49.6 %all-to-all-start.1 = ((bf16[8,16,768]{2,1,0:T(8,128)(2,1)}), bf16[8,16,768]{2,1,0:T(8,128)(2,1)S(1)}, u32[]{:S(2)}, u32[]{:S(2)}) async-start(bf16[8,16,768]{2,1,0:T(8,128)(2,1)} %broadcast_multiply_fusion.2), calls=%async_computation.1 | async-start | bytes 393216 | tf_op jit(solution)/shard_map/all_to_all | solution.py:84
  341.8 198.7 %all-reduce.13.cloned.1.call-start = ((), (), s32[]{:S(2)}) async-start(), calls=%async_computation.6 | async-start | bytes 3670016 | tf_op jit(solution)/shard_map/psum | solution.py:159
  (17 other events, 24.8 us)
Sparse Core Ops, SparseCore 0:
  33.9 76.0 all-reduce.8
  145.6 72.1 all-reduce.10
  409.3 131.1 all-reduce.12
where the time goes:
time: 557 us; the launch traced here: 551 us
  waiting for transfers between devices  238 us (43%)
  local copies, waits for them, and re-layouts  94.4 us (17%)
  blocking collectives  83.3 us (15%)
  matrix products  83.2 us (15%)
  starting transfers between devices  22 us (4%)
  other arithmetic  15.9 us (3%)
  between operations  14.5 us (3%)
    psum x1, waiting for transfers between devices, body(): conv_total, mix_total = lax.psum((conv_part, mix_part), ('dom', 'batch'))  127 us
    psum x2, waiting for transfers between devices, gather_back(): summed = lax.psum(ext_grad[node_dev + halo_count:], 'dom')  110 us
    psum x2, blocking collectives, spread(): hubs = lax.psum(placed, 'dom').astype(jnp.bfloat16)  83.3 us
    dot_general x14, matrix products, mm(): return jnp.dot(left, right, preferred_element_type=jnp.float32)  20.6 us
    dot_general x2, local copies, waits for them, and re-layouts, tile_back(): jnp.einsum('tji,tjf->tif', tile_block, chosen, preferred_element_type=jnp...  13.4 us
    dot_general x2, local copies, waits for them, and re-layouts, tile_apply(): jnp.einsum('tij,tjf->tif', tile_block, chosen, preferred_element_type=jnp...  13.4 us
    unnamed x73, local copies, waits for them, and re-layouts  13.2 us
    all_to_all x2, starting transfers between devices, gather_back(): lax.all_to_all(ext_grad[node_dev:node_dev + halo_count].astype(jnp.bfloat...  11.4 us
  transfers between devices with their start and end apart: 7, of which 3 were waited for; matrix products, arithmetic and copies ran while one was open for 10% of the time, Pallas kernels for 0%

commit v1 on v0

--- a/solution.py
+++ b/solution.py
@@ -156,7 +156,7 @@
     signal_grad = jnp.pad(into_earlier, ((0, 0), (0, 0), (0, 1), (0, 0))) + jnp.pad(
         into_later, ((0, 0), (0, 0), (1, 0), (0, 0))
     )
-    conv_total, mix_total = lax.psum((conv_part, mix_part), ("dom", "batch"))
+    conv_total, mix_total = lax.psum(lax.psum((conv_part, mix_part), "batch"), "dom")
     factor = 1.0 / math.sqrt(
         node_dev * lax.axis_size("dom") * b_dev * lax.axis_size("batch") * out_steps
     )

time: 557 us -> 549 us (0.986)
    psum x1 -> x2, waiting for transfers between devices: 127 us -> 122 us  [the longest x1 79.4 us: body(): lax.psum(lax.psum((conv_part, mix_part), 'batch'), 'dom')]
    unnamed x73 -> x71, local copies, waits for them, and re-layouts: 13.2 us -> 14.2 us
  transfers between devices with their start and end apart: 7 -> 8, of which waited for: 3 -> 5; matrix products, arithmetic and copies ran while one was open for 10% -> 10% of each run, Pallas kernels for 0% -> 0%
where the time goes in v1:
time: 549 us; the launch traced here: 543 us
  waiting for transfers between devices  236 us (43%)
  local copies, waits for them, and re-layouts  95.8 us (17%)
  blocking collectives  82.8 us (15%)
  matrix products  81.2 us (15%)
  starting transfers between devices  18.5 us (3%)
  between operations  14.6 us (3%)
  other arithmetic  13.8 us (3%)
    psum x2, waiting for transfers between devices, gather_back(): summed = lax.psum(ext_grad[node_dev + halo_count:], 'dom')  110 us
    psum x2, blocking collectives, spread(): hubs = lax.psum(placed, 'dom').astype(jnp.bfloat16)  82.8 us
    psum x1, waiting for transfers between devices, body(): lax.psum(lax.psum((conv_part, mix_part), 'batch'), 'dom')  79.4 us
    psum x1, waiting for transfers between devices, body(): lax.psum((conv_part, mix_part), 'batch')  42.5 us
    dot_general x14, matrix products, mm(): return jnp.dot(left, right, preferred_element_type=jnp.float32)  19.3 us
    unnamed x71, local copies, waits for them, and re-layouts  14.2 us
    dot_general x2, local copies, waits for them, and re-layouts, tile_back(): jnp.einsum('tji,tjf->tif', tile_block, chosen, preferred_element_type=jnp...  13.8 us
    dot_general x2, local copies, waits for them, and re-layouts, tile_apply(): jnp.einsum('tij,tjf->tif', tile_block, chosen, preferred_element_type=jnp...  13.7 us
  transfers between devices with their start and end apart: 8, of which 5 were waited for; matrix products, arithmetic and copies ran while one was open for 10% of the time, Pallas kernels for 0%

profile of v1, /device:TPU:0, one launch (start us, length us, event | category | flops | bytes accessed | tf_op | source)
XLA Modules:
  0.0 542.7 jit_solution(10576025521813002492)
XLA Ops:
  13.9 5.6 %fusion.96 = f32[16,768,128]{2,1,0:T(8,128)} fusion(bf16[16,128,768]{2,1,0:T(8,128)(2,1)} %gather_fusion.6, bf16[16,128,128]{2,1,0:T(8,128)(2,1)S(1)} %copy-done), kind=kOutput, calls=%fused_computation.145 | convolution fusion | flops 402653184 | bytes 9961472 | tf_op jit(solution)/shard_map/tji,tjf->tif/dot_general | solution.py:28
  19.6 6.9 %copy.32 = f32[16,768,128]{1,0,2:T(8,128)} copy(f32[16,768,128]{2,1,0:T(8,128)} %fusion.96) | data formatting | bytes 12582912 | tf_op jit(solution)/shard_map/tji,tjf->tif/dot_general | solution.py:28
  26.5 4.6 fusion.2
  36.9 7.3 %all-to-all-start.2 = ((bf16[8,16,768]{2,1,0:T(8,128)(2,1)}), bf16[8,16,768]{2,1,0:T(8,128)(2,1)}, u32[]{:S(2)}, u32[]{:S(2)}) async-start(bf16[8,16,768]{2,1,0:T(8,128)(2,1)} %bitcast.44), calls=%async_computation.2 | async-start | bytes 393216 | tf_op jit(solution)/shard_map/all_to_all | solution.py:98
  61.0 49.2 %all-reduce.11.cloned.1.call-done = f32[128,768]{1,0:T(8,128)} async-done(((f32[128,768]{1,0:T(8,128)}), f32[128,768]{1,0:T(8,128)}) %all-reduce.11.cloned.1.call-update) | async-done | bytes 393232 | tf_op jit(solution)/shard_map/psum | solution.py:105
  125.9 5.6 %fusion.97 = f32[16,768,128]{2,1,0:T(8,128)} fusion(bf16[16,128,768]{2,1,0:T(8,128)(2,1)} %gather_fusion.7, bf16[16,128,128]{2,1,0:T(8,128)(2,1)S(1)} %copy-done), kind=kOutput, calls=%fused_computation.146 | convolution fusion | flops 402653184 | bytes 9961472 | tf_op jit(solution)/shard_map/tji,tjf->tif/dot_general | solution.py:28
  131.5 6.9 %copy.33 = f32[16,768,128]{1,0,2:T(8,128)} copy(f32[16,768,128]{2,1,0:T(8,128)} %fusion.97) | data formatting | bytes 12582912 | tf_op jit(solution)/shard_map/tji,tjf->tif/dot_general | solution.py:28
  138.3 4.6 fusion
  150.3 3.8 all-to-all-start.3
  156.9 60.9 %all-reduce.13.cloned.1.call-done = f32[128,768]{1,0:T(8,128)} async-done(((f32[128,768]{1,0:T(8,128)}), f32[128,768]{1,0:T(8,128)}) %all-reduce.13.cloned.1.call-update) | async-done | bytes 393232 | tf_op jit(solution)/shard_map/psum | solution.py:105
  237.6 40.3 %all-reduce.18 = bf16[128,768]{1,0:T(8,128)(2,1)} all-reduce(f32[128,768]{1,0:T(8,128)S(1)} %convert_select_fusion.1), channel_id=1, replica_groups=mesh['dom'=8,'batch'=4] {'dom'}, use_global_device_ids=true, to_apply=%region_0.1 | all-reduce | flops 98304 | bytes 589824 | tf_op jit(solution)/shard_map/psum | solution.py:88
  286.7 4.0 all-to-all-done
  294.1 5.6 %fusion.94 = f32[16,768,128]{2,1,0:T(8,128)} fusion(bf16[16,128,768]{2,1,0:T(8,128)(2,1)} %gather_fusion.2, bf16[16,128,128]{2,1,0:T(8,128)(2,1)S(1)} %copy-done), kind=kOutput, calls=%fused_computation.143 | convolution fusion | flops 402653184 | bytes 9961472 | tf_op jit(solution)/shard_map/tij,tjf->tif/dot_general | solution.py:14
  299.7 6.9 %copy.30 = f32[16,768,128]{1,0,2:T(8,128)} copy(f32[16,768,128]{2,1,0:T(8,128)} %fusion.94) | data formatting | bytes 12582912 | tf_op jit(solution)/shard_map/tij,tjf->tif/dot_general | solution.py:14
  306.6 5.6 %fusion.26 = bf16[4,128,768]{2,0,1:T(4,128)(2,1)S(1)} fusion(f32[16,768,128]{1,0,2:T(8,128)} %copy.30, f32[16]{0:T(128)S(1)} %convert_element_type.95, s32[16]{0:T(128)S(1)} %copy-done.29), kind=kOutput, calls=%fused_computation.50 | convolution fusion | flops 77463616 | bytes 7078016 | tf_op jit(solution)/shard_map/rt,tif->rif/dot_general | solution.py:19
  320.5 42.5 %all-reduce.19 = bf16[128,768]{1,0:T(8,128)(2,1)} all-reduce(f32[128,768]{1,0:T(8,128)S(1)} %convert_select_fusion), channel_id=1, replica_groups=mesh['dom'=8,'batch'=4] {'dom'}, use_global_device_ids=true, to_apply=%region_1.2 | all-reduce | flops 98304 | bytes 589824 | tf_op jit(solution)/shard_map/psum | solution.py:88
  367.6 5.6 %fusion.95 = f32[16,768,128]{2,1,0:T(8,128)} fusion(bf16[16,128,768]{2,1,0:T(8,128)(2,1)} %gather_fusion.5, bf16[16,128,128]{2,1,0:T(8,128)(2,1)S(1)} %copy-done), kind=kOutput, calls=%fused_computation.144 | convolution fusion | flops 402653184 | bytes 9961472 | tf_op jit(solution)/shard_map/tij,tjf->tif/dot_general | solution.py:14
  373.2 6.9 %copy.31 = f32[16,768,128]{1,0,2:T(8,128)} copy(f32[16,768,128]{2,1,0:T(8,128)} %fusion.95) | data formatting | bytes 12582912 | tf_op jit(solution)/shard_map/tij,tjf->tif/dot_general | solution.py:14
  380.1 5.6 %fusion.29 = bf16[4,128,768]{2,0,1:T(4,128)(2,1)S(1)} fusion(f32[16,768,128]{1,0,2:T(8,128)} %copy.31, f32[16]{0:T(128)S(1)} %convert_element_type.95, s32[16]{0:T(128)S(1)} %copy-done.29), kind=kOutput, calls=%fused_computation.51 | convolution fusion | flops 77463616 | bytes 7078016 | tf_op jit(solution)/shard_map/rt,tif->rif/dot_general | solution.py:19
  390.3 42.5 %all-reduce.17.cloned.1.call-done = (f32[2,2,256,256]{2,3,1,0:T(8,128)}, f32[3,256,256]{2,1,0:T(8,128)}) async-done(((f32[2,2,256,256]{2,3,1,0:T(8,128)}, f32[3,256,256]{2,1,0:T(8,128)}), (f32[2,2,256,256]{2,3,1,0:T(8,128)}, f32[3,256,256]{2,1,0:T(8,128)})) %all-reduce.17.cloned.1.call-update) | async-done | bytes 1835024 | tf_op jit(solution)/shard_map/psum | solution.py:159
  436.0 3.6 reshape.189
  442.4 3.8 reshape.190
  446.1 3.5 fusion.32
  453.0 79.4 %all-reduce.15.cloned.1.call-done = (f32[2,2,256,256]{2,3,1,0:T(8,128)}, f32[3,256,256]{2,1,0:T(8,128)}) async-done(((f32[2,2,256,256]{2,3,1,0:T(8,128)}, f32[3,256,256]{2,1,0:T(8,128)}), (f32[2,2,256,256]{2,3,1,0:T(8,128)}, f32[3,256,256]{2,1,0:T(8,128)})) %all-reduce.15.cloned.1.call-update) | async-done | bytes 1835024 | tf_op jit(solution)/shard_map/psum | solution.py:159
  (170 shorter events, 117.1 us)
Async XLA Ops:
  7.2 6.8 %copy-start = (bf16[16,128,128]{2,1,0:T(8,128)(2,1)S(1)}, bf16[16,128,128]{2,1,0:T(8,128)(2,1)}, u32[]{:S(2)}) copy-start(bf16[16,128,128]{2,1,0:T(8,128)(2,1)} %param.18) | copy-start | bytes 1572868
  7.2 103.0 %all-reduce.11.cloned.1.call-start = ((), (), s32[]{:S(2)}) async-start(), calls=%async_computation.4 | async-start | bytes 786432 | tf_op jit(solution)/shard_map/psum | solution.py:105
  19.6 6.9 %copy-start.30 = (s32[16]{0:T(128)S(1)}, s32[16]{0:T(128)}, u32[]{:S(2)}) copy-start(s32[16]{0:T(128)} %param.21) | copy-start | bytes 196
  19.6 6.9 %copy-start.28 = (s32[16]{0:T(128)S(1)}, s32[16]{0:T(128)}, u32[]{:S(2)}) copy-start(s32[16]{0:T(128)} %param.20) | copy-start | bytes 196
  36.9 76.1 %all-to-all-start.2 = ((bf16[8,16,768]{2,1,0:T(8,128)(2,1)}), bf16[8,16,768]{2,1,0:T(8,128)(2,1)}, u32[]{:S(2)}, u32[]{:S(2)}) async-start(bf16[8,16,768]{2,1,0:T(8,128)(2,1)} %bitcast.44), calls=%async_computation.2 | async-start | bytes 393216 | tf_op jit(solution)/shard_map/all_to_all | solution.py:98
  44.3 173.6 %all-reduce.13.cloned.1.call-start = ((), (), s32[]{:S(2)}) async-start(), calls=%async_computation.5 | async-start | bytes 786432 | tf_op jit(solution)/shard_map/psum | solution.py:105
  44.8 3.4 copy-start.26
  44.8 3.5 copy-start.27
  44.8 3.7 copy-start.25
  44.8 3.7 copy-start.31
  48.7 3.1 copy-start.7
  53.8 5.2 copy-start.16
  56.3 3.1 copy-start.4
  150.3 70.5 %all-to-all-start.3 = ((bf16[8,16,768]{2,1,0:T(8,128)(2,1)}), bf16[8,16,768]{2,1,0:T(8,128)(2,1)S(1)}, u32[]{:S(2)}, u32[]{:S(2)}) async-start(bf16[8,16,768]{2,1,0:T(8,128)(2,1)} %bitcast.46), calls=%async_computation.3 | async-start | bytes 393216 | tf_op jit(solution)/shard_map/all_to_all | solution.py:98
  237.6 45.3 %copy-start.24 = (f32[1,256,256]{1,2,0:T(8,128)S(1)}, f32[1,256,256]{1,2,0:T(8,128)}, u32[]{:S(2)}) copy-start(f32[1,256,256]{1,2,0:T(8,128)} %convolution_bitcast_fusion.4) | copy-start | bytes 786436
  279.5 11.1 %all-to-all-start = ((bf16[8,16,768]{2,1,0:T(8,128)(2,1)}), bf16[8,16,768]{2,1,0:T(8,128)(2,1)S(1)}, u32[]{:S(2)}, u32[]{:S(2)}) async-start(bf16[8,16,768]{2,1,0:T(8,128)(2,1)} %broadcast_multiply_fusion.3), calls=%async_computation | async-start | bytes 393216 | tf_op jit(solution)/shard_map/all_to_all | solution.py:84
  315.0 49.1 %copy-start.14 = (bf16[1536,256]{1,0:T(8,128)(2,1)}, bf16[1536,256]{1,0:T(8,128)(2,1)S(1)}, u32[]{:S(2)}) copy-start(bf16[1536,256]{1,0:T(8,128)(2,1)S(1)} %convert_element_type.97) | copy-start | bytes 2359300
  317.1 47.1 %all-to-all-start.1 = ((bf16[8,16,768]{2,1,0:T(8,128)(2,1)}), bf16[8,16,768]{2,1,0:T(8,128)(2,1)S(1)}, u32[]{:S(2)}, u32[]{:S(2)}) async-start(bf16[8,16,768]{2,1,0:T(8,128)(2,1)} %broadcast_multiply_fusion.2), calls=%async_computation.1 | async-start | bytes 393216 | tf_op jit(solution)/shard_map/all_to_all | solution.py:84
  320.5 112.3 %all-reduce.17.cloned.1.call-start = ((), (), s32[]{:S(2)}) async-start(), calls=%async_computation.7 | async-start | bytes 3670016 | tf_op jit(solution)/shard_map/psum | solution.py:159
  388.1 144.2 %all-reduce.15.cloned.1.call-start = ((), (), s32[]{:S(2)}) async-start(), calls=%async_computation.6 | async-start | bytes 3670016 | tf_op jit(solution)/shard_map/psum | solution.py:159
  442.4 3.8 copy-start.3
  446.1 3.6 copy-start.6
  446.1 3.6 copy-start.11
  446.1 3.6 copy-start.19
  (17 other events, 27.5 us)
Sparse Core Ops, SparseCore 0:
  34.0 76.0 all-reduce.10
  145.9 71.8 all-reduce.12
  388.2 44.5 all-reduce.16
  436.3 95.9 all-reduce.14
